TPU v7x, 32 devices: a whole 2x2x4 slice. The times are simulated.
32 devices in a mesh: ctx: 8 (over z, y), fsdp: 4 (over x, core).
Axes of the slice: x: 2, y: 2, z: 4, core: 2. Of those that a mesh axis runs over, the one named last changes fastest.
Arguments:
- tokens: bfloat16 [4, 1024, 768], P('fsdp', 'ctx'), may hold values from -6 to 6
- first_gain: bfloat16 [768], P('fsdp'), may hold values from 0.5 to 1.5
- first_bias: bfloat16 [768], P('fsdp'), may hold values from -4 to 4
- attn_weight: bfloat16 [768, 2304], P('fsdp'), may hold values from -0.3125 to 0.3125
- query_bias: bfloat16 [768], P('fsdp'), may hold values from -4 to 4
- value_bias: bfloat16 [768], P('fsdp'), may hold values from -4 to 4
- proj_weight: bfloat16 [768, 768], P('fsdp'), may hold values from -6 to 6
- proj_bias: bfloat16 [768], P('fsdp'), may hold values from -6 to 6
- second_gain: bfloat16 [768], P('fsdp'), may hold values from 0.5 to 1.5
- second_bias: bfloat16 [768], P('fsdp'), may hold values from -4 to 4
- fc_weight: bfloat16 [768, 3072], P('fsdp'), may hold values from -0.21875 to 0.21875
- fc_bias: bfloat16 [3072], P('fsdp'), may hold values from -6 to 6
- out_weight: bfloat16 [3072, 768], P('fsdp'), may hold values from -0.3125 to 0.3125
- out_bias: bfloat16 [768], P('fsdp'), may hold values from -6 to 6
- cotangent: bfloat16 [4, 1024, 768], P('fsdp', 'ctx'), may hold values from -6 to 6
Outputs:
- block_out: bfloat16 [4, 1024, 768], P('fsdp', 'ctx')
- input_grad: bfloat16 [4, 1024, 768], P('fsdp', 'ctx')
- first_gain_grad: float32 [768], P('fsdp')
- first_bias_grad: float32 [768], P('fsdp')
- attn_weight_grad: float32 [768, 2304], P('fsdp')
- query_bias_grad: float32 [768], P('fsdp')
- value_bias_grad: float32 [768], P('fsdp')
- proj_weight_grad: float32 [768, 768], P('fsdp')
- proj_bias_grad: float32 [768], P('fsdp')
- second_gain_grad: float32 [768], P('fsdp')
- second_bias_grad: float32 [768], P('fsdp')
- fc_weight_grad: float32 [768, 3072], P('fsdp')
- fc_bias_grad: float32 [3072], P('fsdp')
- out_weight_grad: float32 [3072, 768], P('fsdp')
- out_bias_grad: float32 [768], P('fsdp')
All inputs are finite; a program needn't handle non-finite values.
Results may differ from a plain program's by a relative error of at most 0.017.
Values may be sent and summed in bfloat16 or wider, within the bound.
No kernel may reach another device: no remote copies, remote signals or barrier semaphores. Data moves between devices by JAX's collectives and lax.ppermute only.
A program may use at most 320 MiB of HBM per device.

v0:
```python
from functools import partial
import jax
import jax.numpy as jnp
from jax import lax
from jax.sharding import PartitionSpec as P

D = 768
H = 12
HD = 64
LAYERS = 12
EPSILON = 1e-05


def layer_norm(values_in, norm_gain, norm_shift):
    center = jnp.mean(values_in, axis=-1, keepdims=True)
    centered = values_in - center
    spread = jnp.mean(centered * centered, axis=-1, keepdims=True)
    return centered * lax.rsqrt(spread + EPSILON) * norm_gain + norm_shift


def left_product(first, second):
    return lax.dot_general(
        first, second, (((0,), (0,)), ((), ())), preferred_element_type=jnp.float32
    )


def right_product(first, second):
    return lax.dot_general(
        first, second, (((1,), (1,)), ((), ())), preferred_element_type=jnp.float32
    )


def score_block(query_rows, key_rows, query_offset, key_offset):
    scores = jnp.einsum(
        "sqhd,skhd->shqk", query_rows, key_rows, preferred_element_type=jnp.float32
    ) * HD ** (-0.5)
    query_index = query_offset + lax.broadcasted_iota(jnp.int32, (query_rows.shape[1], 1), 0)
    key_index = key_offset + lax.broadcasted_iota(jnp.int32, (1, key_rows.shape[1]), 1)
    return (scores, (key_index <= query_index)[None, None])


def pair_terms(
    query_rows, grad_rows, log_totals, deltas, key_rows, value_rows, query_offset, key_offset
):
    scores, visible = score_block(query_rows, key_rows, query_offset, key_offset)
    weights = jnp.where(visible, jnp.exp(scores - log_totals[..., None]), 0.0)
    grad_weights = jnp.einsum(
        "sqhd,skhd->shqk", grad_rows, value_rows, preferred_element_type=jnp.float32
    )
    grad_scores = (weights * (grad_weights - deltas[..., None])).astype(jnp.bfloat16)
    return (weights.astype(jnp.bfloat16), grad_scores)


def shards(
    tokens,
    first_gain,
    first_bias,
    attn_weight,
    query_bias,
    value_bias,
    proj_weight,
    proj_bias,
    second_gain,
    second_bias,
    fc_weight,
    fc_bias,
    out_weight,
    out_bias,
    cotangent,
):
    residual_scale = LAYERS ** (-0.5)
    score_scale = HD ** (-0.5)
    seq_count = tokens.shape[0]
    block_rows = tokens.shape[1]
    all_rows = seq_count * block_rows
    inputs = tokens.reshape(all_rows, D).astype(jnp.float32)
    ctx_index = lax.axis_index("ctx")
    my_offset = ctx_index * block_rows
    last_row = my_offset + block_rows - 1
    attn_gathered = (
        lax.all_gather(first_gain, "fsdp", axis=0, tiled=True),
        lax.all_gather(first_bias, "fsdp", axis=0, tiled=True),
        lax.all_gather(attn_weight, "fsdp", axis=0, tiled=True),
        lax.all_gather(query_bias, "fsdp", axis=0, tiled=True),
        lax.all_gather(value_bias, "fsdp", axis=0, tiled=True),
        lax.all_gather(proj_weight, "fsdp", axis=0, tiled=True),
        lax.all_gather(proj_bias, "fsdp", axis=0, tiled=True),
    )
    gain_one, shift_one, attn_matrix, query_shift, value_shift, proj_matrix, proj_shift = (
        attn_gathered
    )
    gain_one = gain_one.astype(jnp.float32)
    shift_one = shift_one.astype(jnp.float32)
    normed = layer_norm(inputs, gain_one, shift_one).astype(jnp.bfloat16)
    mixed_rows = jnp.dot(normed, attn_matrix, preferred_element_type=jnp.float32)
    query_flat = (
        (mixed_rows[:, :D] + query_shift.astype(jnp.float32))
        .astype(jnp.bfloat16)
        .reshape(seq_count, block_rows, D)
    )
    key_flat = mixed_rows[:, D : 2 * D].astype(jnp.bfloat16).reshape(seq_count, block_rows, D)
    value_flat = (
        (mixed_rows[:, 2 * D :] + value_shift.astype(jnp.float32))
        .astype(jnp.bfloat16)
        .reshape(seq_count, block_rows, D)
    )
    query_heads = query_flat.reshape(seq_count, block_rows, H, HD)
    start_state = (
        jnp.full((seq_count, H, block_rows), -1e30, jnp.float32),
        jnp.zeros((seq_count, H, block_rows), jnp.float32),
        jnp.zeros((seq_count, H, block_rows, HD), jnp.float32),
    )
    offset = jnp.int32(0)
    key_rows = lax.all_gather(key_flat, "ctx", axis=1, tiled=True)
    value_rows = lax.all_gather(value_flat, "ctx", axis=1, tiled=True)
    row_count = key_rows.shape[1]

    def update(running):
        running_max, running_sum, running_acc = running
        scores, visible = score_block(
            query_heads, key_rows.reshape(seq_count, row_count, H, HD), my_offset, offset
        )
        scores = jnp.where(visible, scores, -1e30)
        new_max = jnp.maximum(running_max, jnp.max(scores, axis=-1))
        weights = jnp.where(visible, jnp.exp(scores - new_max[..., None]), 0.0)
        running_acc = jnp.einsum(
            "shqk,skhd->shqd",
            weights.astype(jnp.bfloat16),
            value_rows.reshape(seq_count, row_count, H, HD),
            preferred_element_type=jnp.float32,
        )
        running_sum = jnp.sum(weights, axis=-1)
        return (new_max, running_sum, running_acc)

    final_max, final_sum, final_acc = lax.cond(
        offset <= last_row, update, lambda unchanged: unchanged, start_state
    )
    log_totals = final_max + jnp.log(final_sum)
    attended_heads = final_acc / final_sum[..., None]
    attended_exact = attended_heads.transpose(0, 2, 1, 3).reshape(all_rows, D)
    attended = attended_exact.astype(jnp.bfloat16)
    branch = jnp.dot(attended, proj_matrix, preferred_element_type=jnp.float32) + proj_shift.astype(
        jnp.float32
    )
    middle = inputs + residual_scale * branch
    mlp_gathered = (
        lax.all_gather(second_gain, "fsdp", axis=0, tiled=True),
        lax.all_gather(second_bias, "fsdp", axis=0, tiled=True),
        lax.all_gather(fc_weight, "fsdp", axis=0, tiled=True),
        lax.all_gather(fc_bias, "fsdp", axis=0, tiled=True),
        lax.all_gather(out_weight, "fsdp", axis=0, tiled=True),
        lax.all_gather(out_bias, "fsdp", axis=0, tiled=True),
    )
    gain_two, shift_two, fc_matrix, fc_shift, out_matrix, out_shift = mlp_gathered
    gain_two = gain_two.astype(jnp.float32)
    shift_two = shift_two.astype(jnp.float32)
    normed_two = layer_norm(middle, gain_two, shift_two).astype(jnp.bfloat16)
    hidden = jnp.dot(normed_two, fc_matrix, preferred_element_type=jnp.float32) + fc_shift.astype(
        jnp.float32
    )
    gelu_fn = partial(jax.nn.gelu, approximate=True)
    active_exact, gelu_back = jax.vjp(gelu_fn, hidden)
    active = active_exact.astype(jnp.bfloat16)
    output = jnp.dot(active, out_matrix, preferred_element_type=jnp.float32) + out_shift.astype(
        jnp.float32
    )
    block_out = (middle + residual_scale * output).astype(jnp.bfloat16)
    grad_rows = cotangent.reshape(all_rows, D).astype(jnp.float32)
    grad_output = (residual_scale * grad_rows).astype(jnp.bfloat16)
    out_weight_grad = left_product(active, grad_output)
    out_bias_grad = jnp.sum(grad_output.astype(jnp.float32), axis=0)
    grad_active = right_product(grad_output, out_matrix)
    grad_hidden = gelu_back(grad_active)[0].astype(jnp.bfloat16)
    fc_weight_grad = left_product(normed_two, grad_hidden)
    fc_bias_grad = jnp.sum(grad_hidden.astype(jnp.float32), axis=0)
    grad_normed_two = right_product(grad_hidden, fc_matrix)
    norm_two_value, norm_two_back = jax.vjp(layer_norm, middle, gain_two, shift_two)
    grad_middle, second_gain_grad, second_bias_grad = norm_two_back(grad_normed_two)
    grad_middle = grad_middle + grad_rows
    grad_branch = (residual_scale * grad_middle).astype(jnp.bfloat16)
    proj_weight_grad = left_product(attended, grad_branch)
    proj_bias_grad = jnp.sum(grad_branch.astype(jnp.float32), axis=0)
    grad_attended = right_product(grad_branch, proj_matrix).astype(jnp.bfloat16)
    grad_heads = grad_attended.reshape(seq_count, block_rows, H, HD)
    grad_seq = grad_attended.reshape(seq_count, block_rows, D)
    deltas = jnp.sum(grad_heads.astype(jnp.float32).transpose(0, 2, 1, 3) * attended_heads, axis=-1)
    zero_flat = jnp.zeros((seq_count, block_rows, D), jnp.float32)
    zero_heads = jnp.zeros((seq_count, block_rows, H, HD), jnp.float32)
    all_totals, all_deltas = (
        lax.all_gather(log_totals, "ctx", axis=2, tiled=True),
        lax.all_gather(deltas, "ctx", axis=2, tiled=True),
    )
    key_heads_own = key_flat.reshape(seq_count, block_rows, H, HD)
    value_heads_own = value_flat.reshape(seq_count, block_rows, H, HD)

    def key_side(carried, arrived, offset):
        query_rows, grad_piece = arrived
        row_count = query_rows.shape[1]

        def key_visit_block(partials):
            query_part = query_rows.reshape(seq_count, row_count, H, HD)
            grad_part = grad_piece.reshape(seq_count, row_count, H, HD)
            weights, grad_scores = pair_terms(
                query_part,
                grad_part,
                all_totals,
                all_deltas,
                key_heads_own,
                value_heads_own,
                offset,
                my_offset,
            )
            key_sum = score_scale * jnp.einsum(
                "shqk,sqhd->skhd", grad_scores, query_part, preferred_element_type=jnp.float32
            ).reshape(seq_count, block_rows, D)
            value_sum = jnp.einsum(
                "shqk,sqhd->skhd", weights, grad_part, preferred_element_type=jnp.float32
            ).reshape(seq_count, block_rows, D)
            return (key_sum, value_sum)

        return lax.cond(
            offset + row_count - 1 >= my_offset,
            key_visit_block,
            lambda unchanged: unchanged,
            carried,
        )

    key_grad, value_grad = key_side(
        (zero_flat, zero_flat),
        (
            lax.all_gather(query_flat, "ctx", axis=1, tiled=True),
            lax.all_gather(grad_seq, "ctx", axis=1, tiled=True),
        ),
        jnp.int32(0),
    )

    def query_side(carried, arrived, offset):
        key_rows, value_rows = arrived
        row_count = key_rows.shape[1]

        def query_visit_block(query_sum):
            key_part = key_rows.reshape(seq_count, row_count, H, HD)
            weights, grad_scores = pair_terms(
                query_heads,
                grad_heads,
                log_totals,
                deltas,
                key_part,
                value_rows.reshape(seq_count, row_count, H, HD),
                my_offset,
                offset,
            )
            return score_scale * jnp.einsum(
                "shqk,skhd->sqhd", grad_scores, key_part, preferred_element_type=jnp.float32
            )

        return lax.cond(offset <= last_row, query_visit_block, lambda unchanged: unchanged, carried)

    query_grad = query_side(
        zero_heads,
        (
            lax.all_gather(key_flat, "ctx", axis=1, tiled=True),
            lax.all_gather(value_flat, "ctx", axis=1, tiled=True),
        ),
        jnp.int32(0),
    )
    grad_mixed = jnp.concatenate(
        [
            query_grad.reshape(all_rows, D).astype(jnp.bfloat16),
            key_grad.reshape(all_rows, D).astype(jnp.bfloat16),
            value_grad.reshape(all_rows, D).astype(jnp.bfloat16),
        ],
        axis=1,
    )
    attn_weight_grad = left_product(normed, grad_mixed)
    query_bias_grad = jnp.sum(grad_mixed[:, :D].astype(jnp.float32), axis=0)
    value_bias_grad = jnp.sum(grad_mixed[:, 2 * D :].astype(jnp.float32), axis=0)
    grad_normed = right_product(grad_mixed, attn_matrix)
    norm_one_value, norm_one_back = jax.vjp(layer_norm, inputs, gain_one, shift_one)
    grad_inputs, first_gain_grad, first_bias_grad = norm_one_back(grad_normed)
    input_grad = (grad_inputs + grad_middle).astype(jnp.bfloat16)
    owned = (
        lax.psum_scatter(
            first_gain_grad.astype(jnp.bfloat16), "fsdp", scatter_dimension=0, tiled=True
        ).astype(jnp.float32),
        lax.psum_scatter(
            first_bias_grad.astype(jnp.bfloat16), "fsdp", scatter_dimension=0, tiled=True
        ).astype(jnp.float32),
        lax.psum_scatter(
            attn_weight_grad.astype(jnp.bfloat16), "fsdp", scatter_dimension=0, tiled=True
        ).astype(jnp.float32),
        lax.psum_scatter(
            query_bias_grad.astype(jnp.bfloat16), "fsdp", scatter_dimension=0, tiled=True
        ).astype(jnp.float32),
        lax.psum_scatter(
            value_bias_grad.astype(jnp.bfloat16), "fsdp", scatter_dimension=0, tiled=True
        ).astype(jnp.float32),
        lax.psum_scatter(
            proj_weight_grad.astype(jnp.bfloat16), "fsdp", scatter_dimension=0, tiled=True
        ).astype(jnp.float32),
        lax.psum_scatter(
            proj_bias_grad.astype(jnp.bfloat16), "fsdp", scatter_dimension=0, tiled=True
        ).astype(jnp.float32),
        lax.psum_scatter(
            second_gain_grad.astype(jnp.bfloat16), "fsdp", scatter_dimension=0, tiled=True
        ).astype(jnp.float32),
        lax.psum_scatter(
            second_bias_grad.astype(jnp.bfloat16), "fsdp", scatter_dimension=0, tiled=True
        ).astype(jnp.float32),
        lax.psum_scatter(
            fc_weight_grad.astype(jnp.bfloat16), "fsdp", scatter_dimension=0, tiled=True
        ).astype(jnp.float32),
        lax.psum_scatter(
            fc_bias_grad.astype(jnp.bfloat16), "fsdp", scatter_dimension=0, tiled=True
        ).astype(jnp.float32),
        lax.psum_scatter(
            out_weight_grad.astype(jnp.bfloat16), "fsdp", scatter_dimension=0, tiled=True
        ).astype(jnp.float32),
        lax.psum_scatter(
            out_bias_grad.astype(jnp.bfloat16), "fsdp", scatter_dimension=0, tiled=True
        ).astype(jnp.float32),
    )
    summed = lax.psum(
        (
            owned[0],
            owned[1],
            owned[2],
            owned[3],
            owned[4],
            owned[5],
            owned[6],
            owned[7],
            owned[8],
            owned[9],
            owned[10],
            owned[11],
            owned[12],
        ),
        "ctx",
    )
    return (
        block_out.reshape(seq_count, block_rows, D),
        input_grad.reshape(seq_count, block_rows, D),
        summed[0],
        summed[1],
        summed[2],
        summed[3],
        summed[4],
        summed[5],
        summed[6],
        summed[7],
        summed[8],
        summed[9],
        summed[10],
        summed[11],
        summed[12],
    )


def solution(mesh):
    placed = (
        P("fsdp", "ctx", None),
        P("fsdp"),
        P("fsdp"),
        P("fsdp", None),
        P("fsdp"),
        P("fsdp"),
        P("fsdp", None),
        P("fsdp"),
        P("fsdp"),
        P("fsdp"),
        P("fsdp", None),
        P("fsdp"),
        P("fsdp", None),
        P("fsdp"),
        P("fsdp", "ctx", None),
    )
    return jax.shard_map(
        shards,
        mesh=mesh,
        in_specs=placed,
        out_specs=(
            P("fsdp", "ctx", None),
            P("fsdp", "ctx", None),
            P("fsdp"),
            P("fsdp"),
            P("fsdp", None),
            P("fsdp"),
            P("fsdp"),
            P("fsdp", None),
            P("fsdp"),
            P("fsdp"),
            P("fsdp"),
            P("fsdp", None),
            P("fsdp"),
            P("fsdp", None),
            P("fsdp"),
        ),
        check_vma=False,
    )
```

profile of v0, /device:TPU:0, one launch (start us, length us, event | category | flops | bytes accessed | tf_op | source)
XLA Modules:
  0.0 782.9 jit_solution(8197349530382373933)
XLA Ops:
  7.2 0.7 all-gather.15.cloned.1.call-update
  8.0 1.3 fusion.91
  10.0 0.8 dynamic-update-slice
  10.8 0.8 dynamic-update-slice.1
  11.6 0.8 dynamic-update-slice.2
  12.5 0.8 dynamic-update-slice.3
  13.3 0.8 dynamic-update-slice.4
  14.2 0.8 dynamic-update-slice.5
  15.0 0.8 dynamic-update-slice.6
  15.8 13.4 %all-reduce.19 = (bf16[768]{0:T(1024)(128)(2,1)S(1)}, bf16[768]{0:T(1024)(128)(2,1)S(1)}, bf16[768]{0:T(1024)(128)(2,1)S(1)}, bf16[768]{0:T(1024)(128)(2,1)S(1)}...) all-reduce(bf16[768]{0:T(1024)(128)(2,1)S(1)} %dynamic-update-slice, ...), channel_id=1, replica_groups=mesh['ctx'=8,'fsdp'=4] {'fsdp'}, use_global_device_ids=true, to_apply=%add.1 | all-reduce | flops 5376 | bytes 21504
  29.2 1.0 convert_reduce_fusion
  30.3 1.1 fusion.63
  31.4 11.8 %all-gather.15.cloned.1.call-done = bf16[768,2304]{1,0:T(8,128)(2,1)} async-done(((bf16[192,2304]{1,0:T(8,128)(2,1)}), bf16[768,2304]{1,0:T(8,128)(2,1)}) %all-gather.15.cloned.1.call-update) | async-done | bytes 3538960 | tf_op jit(solution)/shard_map/all_gather | solution.py:83
  43.2 2.8 fusion.85
  46.1 0.7 fusion.66
  46.9 0.7 slice.23
  49.5 5.2 all-gather.5
  54.7 0.8 copy.51
  55.7 35.5 %all-gather.25.cloned.1.call-done = bf16[1024,768]{1,0:T(8,128)(2,1)} async-done(((bf16[128,768]{1,0:T(8,128)(2,1)}), bf16[1024,768]{1,0:T(8,128)(2,1)}) %all-gather.25.cloned.1.call-update) | async-done | bytes 1572880 | tf_op jit(solution)/shard_map/all_gather | solution.py:115
  91.3 45.8 %all-gather.23.cloned.1.call-done = bf16[1024,768]{1,0:T(8,128)(2,1)} async-done(((bf16[128,768]{1,0:T(8,128)(2,1)}), bf16[1024,768]{1,0:T(8,128)(2,1)}) %all-gather.23.cloned.1.call-update) | async-done | bytes 1572880 | tf_op jit(solution)/shard_map/all_gather | solution.py:114
  137.1 13.5 %conditional.3 = (f32[1,12,128]{2,1,0:T(8,128)S(1)}, f32[1,12,128,64]{2,3,1,0:T(8,128)S(1)}, f32[1,12,128]{2,1,0:T(8,128)S(1)}) conditional(s32[]{:T(128)} %convert_element_type.215, () %tuple.32, (s32[]{:T(128)}, bf16[1,128,12,64]{1,3,2,0:T(8,128)(2,1)}, bf16[1,1024,768]{2,1,0:T(8,128)(2,1)}, bf16[1,1024,768]{2,1,0:T(8,128)(2,1)}) %tuple.106), branch_computations={%region_2.0_spmd.clone, %region_3.6_spmd.clone} | conditional | flops 423233152 | bytes 60988556 | solution.py:135
  137.2 1.7 copy.61
  138.9 2.2 fusion.26
  141.2 2.0 fusion.28
  143.2 0.8 copy-done
  144.0 1.6 copy.62
  145.6 4.9 fusion.32
  150.6 4.1 all-gather.17.cloned.1.call-done
  154.8 1.7 fusion.92
  156.7 36.9 %all-gather.19.cloned.1.call-done = bf16[768,3072]{1,0:T(8,128)(2,1)} async-done(((bf16[192,3072]{1,0:T(8,128)(2,1)}), bf16[768,3072]{1,0:T(8,128)(2,1)}) %all-gather.19.cloned.1.call-update) | async-done | bytes 4718608 | tf_op jit(solution)/shard_map/all_gather | solution.py:149
  193.7 3.2 convolution_add_fusion
  196.9 35.7 %all-gather.21.cloned.1.call-done = bf16[3072,768]{1,0:T(8,128)(2,1)} async-done(((bf16[768,768]{1,0:T(8,128)(2,1)}), bf16[3072,768]{1,0:T(8,128)(2,1)}) %all-gather.21.cloned.1.call-update) | async-done | bytes 4718608 | tf_op jit(solution)/shard_map/all_gather | solution.py:151
  232.6 5.0 fusion.93
  237.6 2.3 multiply_reduce_fusion
  240.8 0.7 fusion.89
  241.6 1.2 convolution_convert_fusion.4
  242.9 1.5 convolution_convert_fusion.3
  244.4 4.9 convolution_convert_fusion.1
  249.6 3.8 convolution_convert_fusion
  253.5 0.8 copy-done.9
  255.2 17.2 %conditional.4 = (bf16[1,128,12,64]{1,3,2,0:T(8,128)(2,1)S(1)}) conditional(s32[]{:T(128)} %convert_element_type.215, () %tuple.34, (s32[]{:T(128)}, bf16[1,128,12,64]{1,3,2,0:T(8,128)(2,1)}, bf16[1,1024,768]{2,1,0:T(8,128)(2,1)}, f32[1,12,128]{2,1,0:T(8,128)}, bf16[1,128,12,64]{1,3,2,0:T(8,128)(2,1)}, /*index=5*/bf16[1,1024,768]{2,1,0:T(8,128)(2,1)}, ...), branch_computations={%region_11.12_spmd, %region_12.13_spmd} | conditional | flops 613744768 | bytes 25269316 | solution.py:257
  255.2 2.6 copy.55
  257.8 5.2 fusion.8
  263.0 2.6 copy.56
  265.8 6.6 fusion.5
  272.4 32.5 %all-gather.4 = f32[12,1024]{1,0:T(8,128)} all-gather(f32[12,128]{1,0:T(8,128)S(1)} %fusion.68), channel_id=6, replica_groups=mesh['ctx'=8,'fsdp'=4] {'ctx'}, dimensions={1}, use_global_device_ids=true | all-gather | bytes 55296 | tf_op jit(solution)/shard_map/all_gather | solution.py:191
  304.9 33.0 %all_gather.75 = f32[1,12,1024]{2,1,0:T(8,128)} all-gather(f32[1,12,128]{2,1,0:T(8,128)} %copy-done.22), channel_id=1, replica_groups=mesh['ctx'=8,'fsdp'=4] {'ctx'}, dimensions={2}, use_global_device_ids=true | all-gather | bytes 55296 | tf_op jit(solution)/shard_map/all_gather | solution.py:190
  338.0 23.5 %conditional.5 = (bf16[1,128,768]{1,2,0:T(8,128)(2,1)S(1)}, bf16[128,768]{0,1:T(8,128)(2,1)S(1)}) conditional(s32[]{:T(128)} %convert_element_type.242, () %tuple.36, (s32[]{:T(128)}, bf16[1,1024,768]{2,1,0:T(8,128)(2,1)}, bf16[128,768]{1,0:T(8,128)(2,1)S(1)}, f32[1,12,1024]{2,1,0:T(8,128)}, bf16[1,1024,768]{2,1,0:T(8,128)(2,1)}, ...), branch_computations={%region_13.14_spmd, %region_14.15_spmd} | conditional | flops 821362816 | bytes 33965132 | solution.py:221
  338.0 2.6 copy.57
  340.7 5.1 fusion.94
  345.9 2.6 copy.59
  348.7 8.3 %fusion.21 = bf16[12,128,64]{1,2,0:T(8,128)(2,1)S(1)} fusion(bf16[1024,12,64]{0,2,1:T(8,128)(2,1)} %bitcast.164, f32[12,1024,128]{2,1,0:T(8,128)} %fusion.94, f32[12,1024]{1,0:T(8,128)S(1)} %bitcast.189, f32[12,1024]{1,0:T(8,128)} %bitcast.190, pred[1024,128]{1,0:T(8,128)(4,1)S(1)} %iota_compare_fusion.1, bf16[1024,12,64]{0,2,1:T(8,128)(2,1)} %bitcast.176, ...), kind=kOutput, calls=%fused_computation.22 | convolution fusion | flops 412286976 | bytes 10059776 | tf_op jit(solution)/shard_map/cond/branch_1_fun/shqk,sqhd->skhd/dot_general | solution.py:213
  357.0 4.4 fusion.13
  361.5 3.3 convolution_convert_fusion.2
  366.8 1.3 dynamic-update-slice.7
  369.0 0.7 convert_reduce_fusion.1
  369.7 4.1 fusion.88
  374.1 12.4 %all-reduce.18 = (bf16[768]{0:T(1024)(128)(2,1)S(1)}, bf16[768]{0:T(1024)(128)(2,1)S(1)}, bf16[768]{0:T(1024)(128)(2,1)S(1)}, bf16[768]{0:T(1024)(128)(2,1)S(1)}...) all-reduce(bf16[768]{0:T(1024)(128)(2,1)} %dynamic-update-slice.7, ...), channel_id=1, replica_groups=mesh['ctx'=8,'fsdp'=4] {'fsdp'}, use_global_device_ids=true, to_apply=%add.7 | all-reduce | flops 9984 | bytes 39936
  386.9 1.6 fusion.70
  388.5 4.1 fusion.52
  392.6 10.9 %reduce-scatter.9.cloned.1.call-done = bf16[192,3072]{1,0:T(8,128)(2,1)} async-done(((bf16[768,3072]{1,0:T(8,128)(2,1)}), bf16[192,3072]{1,0:T(8,128)(2,1)}) %reduce-scatter.9.cloned.1.call-update) | async-done | bytes 1179664 | tf_op jit(solution)/shard_map/reduce_scatter | solution.py:310
  403.5 50.4 %reduce-scatter.11.cloned.1.call-done = bf16[768,768]{1,0:T(8,128)(2,1)} async-done(((bf16[3072,768]{1,0:T(8,128)(2,1)}), bf16[768,768]{1,0:T(8,128)(2,1)}) %reduce-scatter.11.cloned.1.call-update) | async-done | bytes 1179664 | tf_op jit(solution)/shard_map/reduce_scatter | solution.py:316
  453.9 43.0 %reduce-scatter.5.cloned.1.call-done = bf16[192,2304]{1,0:T(8,128)(2,1)} async-done(((bf16[768,2304]{1,0:T(8,128)(2,1)}), bf16[192,2304]{1,0:T(8,128)(2,1)}) %reduce-scatter.5.cloned.1.call-update) | async-done | bytes 884752 | tf_op jit(solution)/shard_map/reduce_scatter | solution.py:289
  497.0 279.1 %all-reduce.21 = (f32[192]{0:T(256)}, f32[192]{0:T(256)}, f32[192,2304]{1,0:T(8,128)}, f32[192]{0:T(256)}, f32[192]{0:T(256)}, /*index=5*/f32[192,768]{1,0:T(8,1...) all-reduce(f32[192]{0:T(256)S(1)} %get-tuple-element.212, ...), channel_id=1, replica_groups=mesh['ctx'=8,'fsdp'=4] {'ctx'}, use_global_device_ids=true, to_apply=%region_19.20 | all-reduce | flops 1771776 | bytes 10635264 | tf_op jit(solution)/shard_map/psum | solution.py:323
  (145 shorter events, 7.5 us)
Async XLA Ops:
  7.2 36.1 %all-gather.15.cloned.1.call-start = ((), (), s32[]{:S(2)}) async-start(), calls=%async_computation.4 | async-start | bytes 4423680 | tf_op jit(solution)/shard_map/all_gather | solution.py:83
  7.9 83.4 %all-gather.25.cloned.1.call-start = ((), (), s32[]{:S(2)}) async-start(), calls=%async_computation.13 | async-start | bytes 1769472 | tf_op jit(solution)/shard_map/all_gather | solution.py:115
  30.2 15.8 %copy-start.25 = (f32[128]{0:T(128)}, f32[128]{0:T(128)S(1)}, u32[]{:S(2)}) copy-start(f32[128]{0:T(128)S(1)} %broadcast_multiply_fusion.1) | copy-start | bytes 1540
  31.4 14.7 %copy-start.33 = (f32[128]{0:T(128)}, f32[128]{0:T(128)S(1)}, u32[]{:S(2)}) copy-start(f32[128]{0:T(128)S(1)} %fusion.63) | copy-start | bytes 1540
  31.4 14.7 %copy-start.28 = (f32[128]{0:T(128)}, f32[128]{0:T(128)S(1)}, u32[]{:S(2)}) copy-start(f32[128]{0:T(128)S(1)} %fusion.78) | copy-start | bytes 1540
  46.8 7.8 %copy-start.8 = (bf16[128,768]{1,0:T(8,128)(2,1)}, bf16[128,768]{1,0:T(8,128)(2,1)S(1)}, u32[]{:S(2)}) copy-start(bf16[128,768]{1,0:T(8,128)(2,1)S(1)} %get-tuple-element.195) | copy-start | bytes 589828
  46.8 2.6 copy-start.32
  46.9 90.2 %all-gather.23.cloned.1.call-start = ((), (), s32[]{:S(2)}) async-start(), calls=%async_computation.12 | async-start | bytes 1769472 | tf_op jit(solution)/shard_map/all_gather | solution.py:114
  47.6 107.1 %all-gather.17.cloned.1.call-start = ((), (), s32[]{:S(2)}) async-start(), calls=%async_computation.5 | async-start | bytes 1474560 | tf_op jit(solution)/shard_map/all_gather | solution.py:86
  48.2 145.5 %all-gather.19.cloned.1.call-start = ((), (), s32[]{:S(2)}) async-start(), calls=%async_computation.6 | async-start | bytes 5898240 | tf_op jit(solution)/shard_map/all_gather | solution.py:149
  48.8 183.8 %all-gather.21.cloned.1.call-start = ((), (), s32[]{:S(2)}) async-start(), calls=%async_computation.7 | async-start | bytes 5898240 | tf_op jit(solution)/shard_map/all_gather | solution.py:151
  49.4 288.5 %all-gather.27.cloned.1.call-start = ((), (), s32[]{:S(2)}) async-start(), calls=%async_computation.14 | async-start | bytes 1769472 | tf_op jit(solution)/shard_map/all_gather | solution.py:231
  55.5 282.4 %all-gather.29.cloned.1.call-start = ((), (), s32[]{:S(2)}) async-start(), calls=%async_computation.15 | async-start | bytes 1769472 | tf_op jit(solution)/shard_map/all_gather | solution.py:232
  137.1 17.7 %copy-start.2 = (bf16[1,128,768]{2,1,0:T(8,128)(2,1)S(1)}, bf16[1,128,768]{2,1,0:T(8,128)(2,1)}, u32[]{:S(2)}) copy-start(bf16[1,128,768]{2,1,0:T(8,128)(2,1)} %param.21) | copy-start | bytes 589828
  141.2 2.8 copy-start
  141.2 2.8 copy-start.3
  144.0 1.6 copy-start.16
  145.6 5.0 copy-start.17
  150.6 43.1 %copy-start.18 = (f32[1,12,128]{2,1,0:T(8,128)}, f32[1,12,128]{2,1,0:T(8,128)S(1)}, u32[]{:S(2)}) copy-start(f32[1,12,128]{2,1,0:T(8,128)S(1)} %get-tuple-element.81) | copy-start | bytes 18436
  150.6 43.1 %copy-start.22 = (f32[1,12,128]{2,1,0:T(8,128)}, f32[1,12,128]{2,1,0:T(8,128)S(1)}, u32[]{:S(2)}) copy-start(f32[1,12,128]{2,1,0:T(8,128)S(1)} %get-tuple-element.140) | copy-start | bytes 18436
  156.5 83.4 %copy-start.24 = (f32[128]{0:T(128)}, f32[128]{0:T(128)S(1)}, u32[]{:S(2)}) copy-start(f32[128]{0:T(128)S(1)} %broadcast_multiply_fusion) | copy-start | bytes 1540
  156.7 83.2 %copy-start.27 = (f32[128]{0:T(128)}, f32[128]{0:T(128)S(1)}, u32[]{:S(2)}) copy-start(f32[128]{0:T(128)S(1)} %fusion.79) | copy-start | bytes 1540
  193.7 38.9 %copy-start.10 = (bf16[1,128,768]{2,1,0:T(8,128)(2,1)S(1)}, bf16[1,128,768]{2,1,0:T(8,128)(2,1)}, u32[]{:S(2)}) copy-start(bf16[1,128,768]{2,1,0:T(8,128)(2,1)} %param.35) | copy-start | bytes 589828
  232.6 5.1 copy-start.1
  237.6 2.3 copy-start.5
  239.9 1.6 copy-start.4
  240.2 0.6 copy-start.31
  242.8 126.1 %reduce-scatter.7.cloned.1.call-start = ((), (), s32[]{:S(2)}) async-start(), calls=%async_computation.9 | async-start | bytes 1474560 | tf_op jit(solution)/shard_map/reduce_scatter | solution.py:298
  244.4 159.2 %reduce-scatter.9.cloned.1.call-start = ((), (), s32[]{:S(2)}) async-start(), calls=%async_computation.10 | async-start | bytes 5898240 | tf_op jit(solution)/shard_map/reduce_scatter | solution.py:310
  249.3 204.6 %reduce-scatter.11.cloned.1.call-start = ((), (), s32[]{:S(2)}) async-start(), calls=%async_computation.11 | async-start | bytes 5898240 | tf_op jit(solution)/shard_map/reduce_scatter | solution.py:316
  253.4 0.9 copy-start.9
  253.4 1.1 copy-start.19
  253.4 243.6 %reduce-scatter.5.cloned.1.call-start = ((), (), s32[]{:S(2)}) async-start(), calls=%async_computation.8 | async-start | bytes 4423680 | tf_op jit(solution)/shard_map/reduce_scatter | solution.py:289
  254.5 0.7 copy-start.13
  255.2 82.8 %copy-start.6 = (bf16[128,768]{1,0:T(8,128)(2,1)S(1)}, bf16[128,768]{1,0:T(8,128)(2,1)}, u32[]{:S(2)}) copy-start(bf16[128,768]{1,0:T(8,128)(2,1)} %get-tuple-element.194) | copy-start | bytes 589828
  255.2 82.8 %copy-start.7 = (bf16[128,768]{1,0:T(8,128)(2,1)S(1)}, bf16[128,768]{1,0:T(8,128)(2,1)}, u32[]{:S(2)}) copy-start(bf16[128,768]{1,0:T(8,128)(2,1)} %slice.23) | copy-start | bytes 589828
  263.0 2.8 copy-start.14
  263.0 2.8 copy-start.23
  337.9 23.6 %copy-start.26 = (f32[128]{0:T(128)S(1)}, f32[128]{0:T(128)}, u32[]{:S(2)}) copy-start(f32[128]{0:T(128)} %copy-done.25) | copy-start | bytes 1540
  337.9 23.6 %copy-start.29 = (f32[128]{0:T(128)S(1)}, f32[128]{0:T(128)}, u32[]{:S(2)}) copy-start(f32[128]{0:T(128)} %copy-done.28) | copy-start | bytes 1540
  345.9 2.9 copy-start.20
  348.7 8.3 %copy-start.21 = (f32[1,12,1024]{2,1,0:T(8,128)S(1)}, f32[1,12,1024]{2,1,0:T(8,128)}, u32[]{:S(2)}) copy-start(f32[1,12,1024]{2,1,0:T(8,128)} %get-tuple-element.56) | copy-start | bytes 147460 | tf_op jit(solution)/shard_map/cond
  361.5 3.3 copy-start.12
  364.8 1.9 copy-start.35
  369.7 4.1 copy-start.34
  369.7 4.4 copy-start.30
  369.7 17.2 %copy-start.11 = (bf16[1,128,768]{2,1,0:T(8,128)(2,1)S(1)}, bf16[1,128,768]{2,1,0:T(8,128)(2,1)}, u32[]{:S(2)}) copy-start(bf16[1,128,768]{2,1,0:T(8,128)(2,1)} %param.35) | copy-start | bytes 589828
  388.5 108.5 %copy-start.15 = (bf16[192,768]{1,0:T(8,128)(2,1)S(1)}, bf16[192,768]{1,0:T(8,128)(2,1)}, u32[]{:S(2)}) copy-start(bf16[192,768]{1,0:T(8,128)(2,1)} %reduce-scatter.7.cloned.1.call-done) | copy-start | bytes 884740
Sparse Core Ops, SparseCore 0:
  9.6 33.6 all-gather.14
  47.0 44.2 all-gather.24
  94.0 42.9 all-gather.22
  138.5 16.2 all-gather.16
  156.2 37.4 all-gather.18
  195.1 37.4 all-gather.20
  234.8 44.3 all-gather.26
  281.3 43.2 all-gather.28
  327.8 24.7 reduce-scatter.6
  355.1 48.3 reduce-scatter.8
  406.0 47.8 reduce-scatter.10
  456.5 40.4 reduce-scatter.4
where the time goes:
time: 784 us; the launch traced here: 783 us
  blocking collectives  375 us (48%)
  waiting for transfers between devices  277 us (35%)
  matrix products  74.9 us (10%)
  local copies, waits for them, and re-layouts  28.5 us (4%)
  between operations  16.6 us (2%)
  other arithmetic  9.79 us (1%)
    psum x1, blocking collectives, shards(): lax.psum((owned[0], owned[1], owned[2], owned[3], owned[4], owned[5], own...  279 us
    reduce_scatter x1, waiting for transfers between devices, shards(): lax.psum_scatter(out_weight_grad.astype(jnp.bfloat16), 'fsdp', scatter_di...  50.4 us
    all_gather x1, waiting for transfers between devices, shards(): key_rows = lax.all_gather(key_flat, 'ctx', axis=1, tiled=True)  45.8 us
    reduce_scatter x1, waiting for transfers between devices, shards(): lax.psum_scatter(attn_weight_grad.astype(jnp.bfloat16), 'fsdp', scatter_d...  43 us
    all_gather x1, waiting for transfers between devices, shards(): lax.all_gather(fc_weight, 'fsdp', axis=0, tiled=True)  36.9 us
    all_gather x1, waiting for transfers between devices, shards(): lax.all_gather(out_weight, 'fsdp', axis=0, tiled=True)  35.7 us
    all_gather x1, waiting for transfers between devices, shards(): value_rows = lax.all_gather(value_flat, 'ctx', axis=1, tiled=True)  35.5 us
    all_gather x1, blocking collectives, shards(): lax.all_gather(log_totals, 'ctx', axis=2, tiled=True)  33 us
  transfers between devices with their start and end apart: 12, of which 9 were waited for; matrix products, arithmetic and copies ran while one was open for 14% of the time, Pallas kernels for 0%

commit v1 on v0

--- a/solution.py
+++ b/solution.py
@@ -111,8 +111,11 @@
         jnp.zeros((seq_count, H, block_rows, HD), jnp.float32),
     )
     offset = jnp.int32(0)
-    key_rows = lax.all_gather(key_flat, "ctx", axis=1, tiled=True)
-    value_rows = lax.all_gather(value_flat, "ctx", axis=1, tiled=True)
+    key_rows, value_rows = jnp.split(
+        lax.all_gather(jnp.concatenate([key_flat, value_flat], axis=0), "ctx", axis=1, tiled=True),
+        [key_flat.shape[0]],
+        axis=0,
+    )
     row_count = key_rows.shape[1]
 
     def update(running):

time: 784 us -> 848 us (1.082)
  waiting for transfers between devices: 277 us -> 343 us
    all_gather x2 -> x3, waiting for transfers between devices: 81.3 us -> 116 us  [the longest x1 49.7 us: shards(): lax.all_gather(jnp.concatenate([key_flat, value_flat], axis=0), 'ctx', ax...]
    reduce_scatter x1, waiting for transfers between devices: 10.9 us -> 29 us  [shards(): lax.psum_scatter(fc_weight_grad.astype(jnp.bfloat16), 'fsdp', scatter_dim...]
    all_gather x1, waiting for transfers between devices: 0.01 us -> 8.81 us  [shards(): lax.all_gather(grad_seq, 'ctx', axis=1, tiled=True)]
  transfers between devices with their start and end apart: 12 -> 13, of which waited for: 9 -> 12; matrix products, arithmetic and copies ran while one was open for 14% -> 12% of each run, Pallas kernels for 0% -> 0%
where the time goes in v1:
time: 848 us; the launch traced here: 844 us
  blocking collectives  373 us (44%)
  waiting for transfers between devices  343 us (40%)
  matrix products  67 us (8%)
  local copies, waits for them, and re-layouts  27.5 us (3%)
  between operations  16.5 us (2%)
  other arithmetic  15.7 us (2%)
    psum x1, blocking collectives, shards(): lax.psum((owned[0], owned[1], owned[2], owned[3], owned[4], owned[5], own...  279 us
    reduce_scatter x1, waiting for transfers between devices, shards(): lax.psum_scatter(out_weight_grad.astype(jnp.bfloat16), 'fsdp', scatter_di...  50.3 us
    all_gather x1, waiting for transfers between devices, shards(): lax.all_gather(jnp.concatenate([key_flat, value_flat], axis=0), 'ctx', ax...  49.7 us
    all_gather x1, waiting for transfers between devices, shards(): lax.all_gather(value_flat, 'ctx', axis=1, tiled=True)  45.2 us
    reduce_scatter x1, waiting for transfers between devices, shards(): lax.psum_scatter(attn_weight_grad.astype(jnp.bfloat16), 'fsdp', scatter_d...  43.2 us
    all_gather x1, waiting for transfers between devices, shards(): lax.all_gather(fc_weight, 'fsdp', axis=0, tiled=True)  36.9 us
    all_gather x1, waiting for transfers between devices, shards(): lax.all_gather(out_weight, 'fsdp', axis=0, tiled=True)  35.7 us
    all_gather x1, blocking collectives, shards(): lax.all_gather(deltas, 'ctx', axis=2, tiled=True)  32.9 us
  transfers between devices with their start and end apart: 13, of which 12 were waited for; matrix products, arithmetic and copies ran while one was open for 12% of the time, Pallas kernels for 0%

profile of v1, /device:TPU:0, one launch (start us, length us, event | category | flops | bytes accessed | tf_op | source)
XLA Modules:
  0.0 844.0 jit_solution(9345894214068369178)
XLA Ops:
  8.0 1.3 fusion.92
  10.0 0.8 dynamic-update-slice.1
  10.8 0.8 dynamic-update-slice
  11.6 0.8 dynamic-update-slice.2
  12.5 0.8 dynamic-update-slice.3
  13.3 0.8 dynamic-update-slice.4
  14.2 0.8 dynamic-update-slice.6
  15.0 0.8 dynamic-update-slice.5
  15.8 13.4 %all-reduce.19 = (bf16[768]{0:T(1024)(128)(2,1)S(1)}, bf16[768]{0:T(1024)(128)(2,1)S(1)}, bf16[768]{0:T(1024)(128)(2,1)S(1)}, bf16[768]{0:T(1024)(128)(2,1)S(1)}...) all-reduce(bf16[768]{0:T(1024)(128)(2,1)S(1)} %dynamic-update-slice, ...), channel_id=1, replica_groups=mesh['ctx'=8,'fsdp'=4] {'fsdp'}, use_global_device_ids=true, to_apply=%add.1 | all-reduce | flops 5376 | bytes 21504
  29.2 1.0 convert_reduce_fusion
  30.3 1.1 fusion.63
  31.4 11.8 %all-gather.16.cloned.1.call-done = bf16[768,2304]{1,0:T(8,128)(2,1)} async-done(((bf16[192,2304]{1,0:T(8,128)(2,1)}), bf16[768,2304]{1,0:T(8,128)(2,1)}) %all-gather.16.cloned.1.call-update) | async-done | bytes 3538960 | tf_op jit(solution)/shard_map/all_gather | solution.py:83
  43.2 2.8 fusion.85
  46.2 0.9 pad_maximum_fusion.1
  51.2 5.2 all-gather.5
  57.0 0.8 copy.49
  58.1 49.7 %all-gather.18.cloned.1.call-done = bf16[2,1024,768]{2,1,0:T(8,128)(2,1)} async-done(((bf16[2,128,768]{2,1,0:T(8,128)(2,1)}), bf16[2,1024,768]{2,1,0:T(8,128)(2,1)}) %all-gather.18.cloned.1.call-update) | async-done | bytes 3145744 | tf_op jit(solution)/shard_map/all_gather | solution.py:115
  107.8 11.9 %conditional.3 = (f32[1,12,128]{2,1,0:T(8,128)}, f32[1,12,128,64]{2,3,1,0:T(8,128)}, f32[1,12,128]{2,1,0:T(8,128)S(1)}) conditional(s32[]{:T(128)} %convert_element_type.215, () %tuple.32, (s32[]{:T(128)}, bf16[1,128,12,64]{1,3,2,0:T(8,128)(2,1)}, bf16[2,1024,768]{2,1,0:T(8,128)(2,1)}) %tuple.33), branch_computations={%region_2.0_spmd.clone, %region_3.6_spmd.clone} | conditional | flops 423233152 | bytes 35773468 | solution.py:138
  108.0 3.2 copy.58
  111.5 2.3 fusion.26
  113.8 2.6 fusion.28
  116.4 2.6 fusion.32
  120.3 1.0 fusion.71
  121.3 4.2 all-gather.20.cloned.1.call-done
  125.5 1.7 fusion.93
  127.5 36.9 %all-gather.22.cloned.1.call-done = bf16[768,3072]{1,0:T(8,128)(2,1)} async-done(((bf16[192,3072]{1,0:T(8,128)(2,1)}), bf16[768,3072]{1,0:T(8,128)(2,1)}) %all-gather.22.cloned.1.call-update) | async-done | bytes 4718608 | tf_op jit(solution)/shard_map/all_gather | solution.py:152
  164.4 3.2 convolution_add_fusion
  167.6 35.7 %all-gather.24.cloned.1.call-done = bf16[3072,768]{1,0:T(8,128)(2,1)} async-done(((bf16[768,768]{1,0:T(8,128)(2,1)}), bf16[3072,768]{1,0:T(8,128)(2,1)}) %all-gather.24.cloned.1.call-update) | async-done | bytes 4718608 | tf_op jit(solution)/shard_map/all_gather | solution.py:154
  203.3 5.1 fusion.94
  208.4 2.3 multiply_reduce_fusion
  210.7 1.0 fusion.90
  213.2 1.2 convolution_convert_fusion.4
  214.5 2.4 convolution_convert_fusion.3
  216.9 4.4 convolution_convert_fusion.1
  222.2 3.8 convolution_convert_fusion
  226.1 0.9 copy-done.8
  227.1 1.1 fusion.68
  228.2 21.3 %all-gather.26.cloned.1.call-done = bf16[1024,768]{1,0:T(8,128)(2,1)} async-done(((bf16[128,768]{1,0:T(8,128)(2,1)}), bf16[1024,768]{1,0:T(8,128)(2,1)}) %all-gather.26.cloned.1.call-update) | async-done | bytes 1572880 | tf_op jit(solution)/shard_map/all_gather | solution.py:265
  249.6 45.2 %all-gather.28.cloned.1.call-done = bf16[1024,768]{1,0:T(8,128)(2,1)} async-done(((bf16[128,768]{1,0:T(8,128)(2,1)}), bf16[1024,768]{1,0:T(8,128)(2,1)}) %all-gather.28.cloned.1.call-update) | async-done | bytes 1572880 | tf_op jit(solution)/shard_map/all_gather | solution.py:266
  294.8 17.9 %conditional.4 = (bf16[1,128,12,64]{1,3,2,0:T(8,128)(2,1)S(1)}) conditional(s32[]{:T(128)} %convert_element_type.215, () %tuple.34, (s32[]{:T(128)}, bf16[1,128,12,64]{1,3,2,0:T(8,128)(2,1)}, bf16[1,1024,768]{2,1,0:T(8,128)(2,1)}, f32[1,12,128]{2,1,0:T(8,128)}, bf16[1,128,12,64]{1,3,2,0:T(8,128)(2,1)}, /*index=5*/bf16[1,1024,768]{2,1,0:T(8,128)(2,1)}, ...), branch_computations={%region_11.12_spmd, %region_12.13_spmd} | conditional | flops 613744768 | bytes 25244712 | solution.py:260
  294.8 2.6 copy.52
  297.4 5.2 fusion.8
  302.6 0.8 iota_compare_fusion
  303.4 2.6 copy.53
  306.1 6.7 fusion.5
  312.7 32.0 %all_gather.77 = f32[1,12,1024]{2,1,0:T(8,128)} all-gather(f32[1,12,128]{2,1,0:T(8,128)} %copy-done.21), channel_id=1, replica_groups=mesh['ctx'=8,'fsdp'=4] {'ctx'}, dimensions={2}, use_global_device_ids=true | all-gather | bytes 55296 | tf_op jit(solution)/shard_map/all_gather | solution.py:193
  344.7 32.9 %all-gather.4 = f32[12,1024]{1,0:T(8,128)} all-gather(f32[12,128]{1,0:T(8,128)S(1)} %fusion.68), channel_id=6, replica_groups=mesh['ctx'=8,'fsdp'=4] {'ctx'}, dimensions={1}, use_global_device_ids=true | all-gather | bytes 55296 | tf_op jit(solution)/shard_map/all_gather | solution.py:194
  377.6 8.8 %all-gather.32.cloned.1.call-done = bf16[1024,768]{1,0:T(8,128)(2,1)} async-done(((bf16[128,768]{1,0:T(8,128)(2,1)}), bf16[1024,768]{1,0:T(8,128)(2,1)}) %all-gather.32.cloned.1.call-update) | async-done | bytes 1572880 | tf_op jit(solution)/shard_map/all_gather | solution.py:235
  386.5 19.1 %conditional.5 = (bf16[1,128,768]{1,2,0:T(8,128)(2,1)S(1)}, bf16[128,768]{0,1:T(8,128)(2,1)S(1)}) conditional(s32[]{:T(128)} %convert_element_type.242, () %tuple.36, (s32[]{:T(128)}, bf16[1,1024,768]{2,1,0:T(8,128)(2,1)}, bf16[128,768]{1,0:T(8,128)(2,1)S(1)}, f32[1,12,1024]{2,1,0:T(8,128)}, bf16[1,1024,768]{2,1,0:T(8,128)(2,1)}, ...), branch_computations={%region_13.14_spmd, %region_14.15_spmd} | conditional | flops 821362816 | bytes 65750148 | solution.py:224
  386.5 2.6 copy.56
  389.1 2.6 copy.54
  391.8 2.6 fusion.95
  394.6 2.0 fusion.13
  397.3 8.2 fusion.21
  405.6 3.0 convolution_convert_fusion.2
  410.4 3.6 reduce-scatter.7.cloned.1.call-done
  414.3 3.4 fusion.88
  418.8 10.5 %all-reduce.18 = (bf16[768]{0:T(1024)(128)(2,1)S(1)}, bf16[768]{0:T(1024)(128)(2,1)S(1)}, bf16[768]{0:T(1024)(128)(2,1)S(1)}, bf16[768]{0:T(1024)(128)(2,1)S(1)}...) all-reduce(bf16[768]{0:T(1024)(128)(2,1)S(1)} %dynamic-update-slice, ...), channel_id=1, replica_groups=mesh['ctx'=8,'fsdp'=4] {'fsdp'}, use_global_device_ids=true, to_apply=%add.7 | all-reduce | flops 9984 | bytes 39936
  429.6 1.9 fusion.70
  431.5 4.1 fusion.52
  435.7 29.0 %reduce-scatter.9.cloned.1.call-done = bf16[192,3072]{1,0:T(8,128)(2,1)} async-done(((bf16[768,3072]{1,0:T(8,128)(2,1)}), bf16[192,3072]{1,0:T(8,128)(2,1)}) %reduce-scatter.9.cloned.1.call-update) | async-done | bytes 1179664 | tf_op jit(solution)/shard_map/reduce_scatter | solution.py:313
  464.7 50.3 %reduce-scatter.11.cloned.1.call-done = bf16[768,768]{1,0:T(8,128)(2,1)} async-done(((bf16[3072,768]{1,0:T(8,128)(2,1)}), bf16[768,768]{1,0:T(8,128)(2,1)}) %reduce-scatter.11.cloned.1.call-update) | async-done | bytes 1179664 | tf_op jit(solution)/shard_map/reduce_scatter | solution.py:319
  515.0 43.2 %reduce-scatter.5.cloned.1.call-done = bf16[192,2304]{1,0:T(8,128)(2,1)} async-done(((bf16[768,2304]{1,0:T(8,128)(2,1)}), bf16[192,2304]{1,0:T(8,128)(2,1)}) %reduce-scatter.5.cloned.1.call-update) | async-done | bytes 884752 | tf_op jit(solution)/shard_map/reduce_scatter | solution.py:292
  558.2 279.0 %all-reduce.21 = (f32[192]{0:T(256)}, f32[192]{0:T(256)}, f32[192,2304]{1,0:T(8,128)}, f32[192]{0:T(256)}, f32[192]{0:T(256)}, /*index=5*/f32[192,768]{1,0:T(8,1...) all-reduce(f32[192]{0:T(256)S(1)} %get-tuple-element.210, ...), channel_id=1, replica_groups=mesh['ctx'=8,'fsdp'=4] {'ctx'}, use_global_device_ids=true, to_apply=%region_19.20 | all-reduce | flops 1771776 | bytes 10635264 | tf_op jit(solution)/shard_map/psum | solution.py:326
  (156 shorter events, 13.6 us)
Async XLA Ops:
  7.2 36.1 %all-gather.16.cloned.1.call-start = ((), (), s32[]{:S(2)}) async-start(), calls=%async_computation.4 | async-start | bytes 4423680 | tf_op jit(solution)/shard_map/all_gather | solution.py:83
  7.9 99.9 %all-gather.18.cloned.1.call-start = ((), (), s32[]{:S(2)}) async-start(), calls=%async_computation.5 | async-start | bytes 3538944 | tf_op jit(solution)/shard_map/all_gather | solution.py:115
  30.2 15.8 %copy-start.23 = (f32[128]{0:T(128)}, f32[128]{0:T(128)S(1)}, u32[]{:S(2)}) copy-start(f32[128]{0:T(128)S(1)} %broadcast_multiply_fusion.1) | copy-start | bytes 1540
  31.4 14.7 %copy-start.36 = (f32[128]{0:T(128)}, f32[128]{0:T(128)S(1)}, u32[]{:S(2)}) copy-start(f32[128]{0:T(128)S(1)} %fusion.63) | copy-start | bytes 1540
  31.4 14.7 %copy-start.26 = (f32[128]{0:T(128)}, f32[128]{0:T(128)S(1)}, u32[]{:S(2)}) copy-start(f32[128]{0:T(128)S(1)} %fusion.78) | copy-start | bytes 1540
  46.2 2.9 copy-start.4
  46.2 10.8 %copy-start.6 = (bf16[128,768]{1,0:T(8,128)(2,1)}, bf16[128,768]{1,0:T(8,128)(2,1)S(1)}, u32[]{:S(2)}) copy-start(bf16[128,768]{1,0:T(8,128)(2,1)S(1)} %get-tuple-element.193) | copy-start | bytes 589828
  47.1 78.4 %all-gather.20.cloned.1.call-start = ((), (), s32[]{:S(2)}) async-start(), calls=%async_computation.6 | async-start | bytes 1474560 | tf_op jit(solution)/shard_map/all_gather | solution.py:86
  47.8 3.4 copy-start.35
  47.9 116.5 %all-gather.22.cloned.1.call-start = ((), (), s32[]{:S(2)}) async-start(), calls=%async_computation.7 | async-start | bytes 5898240 | tf_op jit(solution)/shard_map/all_gather | solution.py:152
  48.4 154.9 %all-gather.24.cloned.1.call-start = ((), (), s32[]{:S(2)}) async-start(), calls=%async_computation.8 | async-start | bytes 5898240 | tf_op jit(solution)/shard_map/all_gather | solution.py:154
  49.0 200.5 %all-gather.26.cloned.1.call-start = ((), (), s32[]{:S(2)}) async-start(), calls=%async_computation.13 | async-start | bytes 1769472 | tf_op jit(solution)/shard_map/all_gather | solution.py:265
  49.8 245.0 %all-gather.28.cloned.1.call-start = ((), (), s32[]{:S(2)}) async-start(), calls=%async_computation.14 | async-start | bytes 1769472 | tf_op jit(solution)/shard_map/all_gather | solution.py:266
  50.6 327.1 %all-gather.30.cloned.1.call-start = ((), (), s32[]{:S(2)}) async-start(), calls=%async_computation.15 | async-start | bytes 1769472 | tf_op jit(solution)/shard_map/all_gather | solution.py:234
  57.8 328.6 %all-gather.32.cloned.1.call-start = ((), (), s32[]{:S(2)}) async-start(), calls=%async_computation.16 | async-start | bytes 1769472 | tf_op jit(solution)/shard_map/all_gather | solution.py:235
  107.8 17.7 %copy-start.1 = (bf16[1,128,768]{2,1,0:T(8,128)(2,1)S(1)}, bf16[1,128,768]{2,1,0:T(8,128)(2,1)}, u32[]{:S(2)}) copy-start(bf16[1,128,768]{2,1,0:T(8,128)(2,1)} %param.21) | copy-start | bytes 589828
  119.7 0.6 copy-start.21
  119.7 44.7 %copy-start.20 = (f32[4,1,768]{2,1,0:T(1,128)S(1)}, f32[4,1,768]{2,1,0:T(1,128)}, u32[]{:S(2)}) copy-start(f32[4,1,768]{2,1,0:T(1,128)} %convert_element_type.268) | copy-start | bytes 36868
  127.2 81.1 %copy-start.22 = (f32[128]{0:T(128)}, f32[128]{0:T(128)S(1)}, u32[]{:S(2)}) copy-start(f32[128]{0:T(128)S(1)} %broadcast_multiply_fusion) | copy-start | bytes 1540
  127.4 80.9 %copy-start.25 = (f32[128]{0:T(128)}, f32[128]{0:T(128)S(1)}, u32[]{:S(2)}) copy-start(f32[128]{0:T(128)S(1)} %fusion.79) | copy-start | bytes 1540
  164.4 38.9 %copy-start.10 = (bf16[1,128,768]{2,1,0:T(8,128)(2,1)S(1)}, bf16[1,128,768]{2,1,0:T(8,128)(2,1)}, u32[]{:S(2)}) copy-start(bf16[1,128,768]{2,1,0:T(8,128)(2,1)} %param.35) | copy-start | bytes 589828
  203.3 5.1 copy-start
  208.4 3.4 copy-start.11
  210.7 2.5 copy-start.3
  211.7 0.8 copy-start.33
  212.5 0.7 copy-start.9
  214.4 199.7 %reduce-scatter.7.cloned.1.call-start = ((), (), s32[]{:S(2)}) async-start(), calls=%async_computation.10 | async-start | bytes 1474560 | tf_op jit(solution)/shard_map/reduce_scatter | solution.py:301
  216.9 247.8 %reduce-scatter.9.cloned.1.call-start = ((), (), s32[]{:S(2)}) async-start(), calls=%async_computation.11 | async-start | bytes 5898240 | tf_op jit(solution)/shard_map/reduce_scatter | solution.py:313
  221.3 0.9 copy-start.12
  221.3 293.7 %reduce-scatter.11.cloned.1.call-start = ((), (), s32[]{:S(2)}) async-start(), calls=%async_computation.12 | async-start | bytes 5898240 | tf_op jit(solution)/shard_map/reduce_scatter | solution.py:319
  226.0 0.9 copy-start.8
  226.0 332.2 %reduce-scatter.5.cloned.1.call-start = ((), (), s32[]{:S(2)}) async-start(), calls=%async_computation.9 | async-start | bytes 4423680 | tf_op jit(solution)/shard_map/reduce_scatter | solution.py:292
  227.1 67.7 %copy-start.15 = (bf16[128,768]{0,1:T(8,128)(2,1)}, bf16[128,768]{0,1:T(8,128)(2,1)S(1)}, u32[]{:S(2)}) copy-start(bf16[128,768]{0,1:T(8,128)(2,1)S(1)} %copy.51) | copy-start | bytes 589828
  294.8 91.7 %copy-start.5 = (bf16[128,768]{1,0:T(8,128)(2,1)S(1)}, bf16[128,768]{1,0:T(8,128)(2,1)}, u32[]{:S(2)}) copy-start(bf16[128,768]{1,0:T(8,128)(2,1)} %copy-done.4) | copy-start | bytes 589828
  294.8 91.7 %copy-start.7 = (bf16[128,768]{1,0:T(8,128)(2,1)S(1)}, bf16[128,768]{1,0:T(8,128)(2,1)}, u32[]{:S(2)}) copy-start(bf16[128,768]{1,0:T(8,128)(2,1)} %slice.23) | copy-start | bytes 589828
  303.4 2.6 copy-start.16
  386.5 19.1 %copy-start.24 = (f32[128]{0:T(128)S(1)}, f32[128]{0:T(128)}, u32[]{:S(2)}) copy-start(f32[128]{0:T(128)} %copy-done.23) | copy-start | bytes 1540
  386.5 19.1 %copy-start.27 = (f32[128]{0:T(128)S(1)}, f32[128]{0:T(128)}, u32[]{:S(2)}) copy-start(f32[128]{0:T(128)} %copy-done.26) | copy-start | bytes 1540
  391.8 2.8 copy-start.13
  391.8 2.8 copy-start.19
  394.4 2.7 copy-start.2
  394.6 2.6 copy-start.18
  408.6 1.3 copy-start.38
  414.2 3.5 copy-start.37
  414.2 4.5 copy-start.28
  414.2 4.5 copy-start.29
  414.2 4.5 copy-start.30
  414.3 4.5 copy-start.31
  414.3 4.5 copy-start.32
  414.3 15.4 %copy-start.34 = (f32[128]{0:T(128)S(1)}, f32[128]{0:T(128)}, u32[]{:S(2)}) copy-start(f32[128]{0:T(128)} %copy-done.33) | copy-start | bytes 1540
  417.7 0.8 copy-start.14
  431.5 126.7 %copy-start.17 = (bf16[192,768]{1,0:T(8,128)(2,1)S(1)}, bf16[192,768]{1,0:T(8,128)(2,1)}, u32[]{:S(2)}) copy-start(bf16[192,768]{1,0:T(8,128)(2,1)} %reduce-scatter.7.cloned.1.call-done) | copy-start | bytes 884740
Sparse Core Ops, SparseCore 0:
  9.6 33.6 all-gather.15
  47.2 60.5 all-gather.17
  109.4 16.0 all-gather.19
  126.9 37.4 all-gather.21
  165.8 37.4 all-gather.23
  205.3 44.1 all-gather.25
  251.7 42.9 all-gather.27
  297.5 43.3 all-gather.29
  343.1 43.3 all-gather.31
  389.4 24.5 reduce-scatter.6
  416.8 47.8 reduce-scatter.8
  467.1 47.8 reduce-scatter.10
  517.7 40.4 reduce-scatter.4
